TPU v7x, 256 devices: a whole 4x4x8 slice. The times are simulated.
256 devices in a mesh: gx: 8 (over y, core), gy: 32 (over x, z).
Axes of the slice: x: 4, y: 4, z: 8, core: 2. Of those that a mesh axis runs over, the one named last changes fastest.
Arguments:
- control: float32 [1, 2, 6, 1536, 3072], P(None, None, None, 'gy', 'gx'), may hold values from -6 to 6
- sigma: float32 [2, 6, 1536, 3072], P(None, None, 'gy', 'gx'), may hold values from 0.5 to 5
- kappa: float32 [5, 1536, 3072], P(None, 'gy', 'gx'), may hold values from 0.05 to 5
- beta: float32 [6, 1536, 3072], P(None, 'gy', 'gx'), may hold values from -3 to 3
- sea_mask: int32 [1536, 3072], P('gy', 'gx'), may hold values 0 or 1
- x_inverse: float32 [3072, 3072], P('gx'), as said below
- y_inverse: float32 [1536, 1536], P('gx')
- ssh_coef: float32 [2, 6], replicated, may hold values from -1.5 to 1.5
- obs_owner: int32 [65536, 1], P(('gx', 'gy')), may hold values from 0 to 255; in each aligned block of 256 rows (0 to 255, 256 to 511, ...) at most 2 rows name the same one
- tile_index: int32 [65536], P(('gx', 'gy')), may hold values from 0 to 18046, as said below
- obs_frac: float32 [2, 65536], P(None, ('gx', 'gy')), may hold values from 0 to 1
- obs_count: int32 [256], P(('gx', 'gy')), may hold values from 128 to 256
Outputs:
- increments: float32 [1, 2, 6, 1536, 3072], P(None, None, None, 'gy', 'gx')
- sea_height: float32 [1, 1536, 3072], P(None, 'gy', 'gx')
- obs_equiv: float32 [2, 13, 65536], P(None, None, ('gx', 'gy'))
Inputs may be any that keep to these rules, and one draw needn't show every extreme that they name: `obs_owner`: among the slots of one device, at most 2 name the same owner. `tile_index`: row * 384 + column of a cell in the device's own tile, with row below 47 and column below 383. `x_inverse`: the zonal inverse is symmetric.
All inputs are finite; a program needn't handle non-finite values. No bound on the sum of `sea_mask` on one device may be relied on, other than what follows from the above.
Results may differ from a plain program's by a relative error of at most 0.00013.
Values sent between devices are 32-bit elements; how exact they have to be, the bound alone decides.
A program may use at most 128 MiB of HBM per device.

v0:
```python
import jax
import jax.numpy as jnp
from jax import lax
from jax.sharding import PartitionSpec as P

STEPS = 2
CAP = 2


def vertical(values, kappa):
    levels = values.shape[2]
    c_list = []
    d_list = []
    for level in range(levels):
        k_below = kappa[level - 1] if level > 0 else 0.0
        k_above = kappa[level] if level < levels - 1 else 0.0
        diag_term = 1.0 + k_below + k_above
        if level == 0:
            pivot = diag_term
            d_new = values[:, :, 0] / pivot
        else:
            pivot = diag_term + k_below * c_list[-1]
            d_new = (values[:, :, level] + k_below * d_list[-1]) / pivot
        c_list.append(-k_above / pivot)
        d_list.append(d_new)
    result = [d_list[-1]]
    for level in range(levels - 2, -1, -1):
        result.insert(0, d_list[level] - c_list[level] * result[0])
    return jnp.stack(result, axis=2)


def body(
    control,
    sigma,
    kappa,
    beta,
    sea_mask,
    x_inverse,
    y_inverse,
    ssh_coef,
    obs_owner,
    tile_index,
    obs_frac,
    obs_count,
):
    highest = lax.Precision.HIGHEST
    vec_count, kinds, levels, lat_rows, lon_cols = control.shape
    field_count = vec_count * kinds * levels
    sea_open = sea_mask.astype(jnp.float32)
    grid_field = control.reshape(field_count, lat_rows, lon_cols)
    whole_y = lax.all_gather(y_inverse, "gx", axis=0, tiled=True)
    for diffusion_step in range(STEPS):
        grid_field = sea_open * jnp.einsum(
            "fyb,ab->fya",
            lax.all_gather(grid_field, "gx", axis=2, tiled=True),
            x_inverse,
            precision=highest,
        )
        turned = jnp.swapaxes(grid_field, 1, 2)
        merid_lines = lax.all_to_all(turned, "gy", split_axis=1, concat_axis=2, tiled=True)
        solved = jnp.einsum("fxb,ab->fxa", merid_lines, whole_y, precision=highest)
        returned = lax.all_to_all(solved, "gy", split_axis=2, concat_axis=1, tiled=True)
        grid_field = sea_open * jnp.swapaxes(returned, 1, 2)
        grid_field = vertical(
            grid_field.reshape(vec_count, kinds, levels, lat_rows, lon_cols), kappa
        ).reshape(field_count, lat_rows, lon_cols)
    grid_field = grid_field.reshape(vec_count, kinds, levels, lat_rows, lon_cols)
    temper = sigma[0] * grid_field[:, 0]
    saline = sigma[1] * grid_field[:, 1] + beta * temper
    height = jnp.sum(
        ssh_coef[0][None, :, None, None] * temper + ssh_coef[1][None, :, None, None] * saline,
        axis=1,
    )
    increments = jnp.stack([temper, saline], axis=1)
    profile = jnp.concatenate([temper, saline, height[:, None]], axis=1)
    slot_total = tile_index.shape[0]
    row_index = tile_index // lon_cols
    col_index = tile_index % lon_cols
    frac_x = obs_frac[0]
    frac_y = obs_frac[1]
    corner_a = profile[:, :, row_index, col_index]
    corner_b = profile[:, :, row_index, col_index + 1]
    corner_c = profile[:, :, row_index + 1, col_index]
    corner_d = profile[:, :, row_index + 1, col_index + 1]
    interp = (1.0 - frac_y) * ((1.0 - frac_x) * corner_a + frac_x * corner_b) + frac_y * (
        (1.0 - frac_x) * corner_c + frac_x * corner_d
    )
    live_slot = (jnp.arange(slot_total, dtype=jnp.int32) < obs_count[0]).astype(jnp.float32)
    record_len = interp.shape[0] * interp.shape[1]
    interp = (interp * live_slot).reshape(record_len, slot_total)
    gx_count = lax.axis_size("gx")
    gy_count = lax.axis_size("gy")
    device_total = gx_count * gy_count
    owners = obs_owner[:, 0]
    one_hot = (owners[:, None] == jnp.arange(device_total, dtype=jnp.int32)[None, :]).astype(
        jnp.int32
    )
    before = jnp.cumsum(one_hot, axis=0) - one_hot
    slot_rank = jnp.sum(before * one_hot, axis=1)
    outgoing = (
        jnp.zeros((CAP, record_len, device_total), jnp.float32)
        .at[slot_rank, :, owners]
        .set(interp.T)
    )
    outgoing = outgoing.reshape(CAP, record_len, gx_count, gy_count)
    arrived = lax.all_to_all(
        lax.all_to_all(outgoing, "gx", split_axis=2, concat_axis=2, tiled=True),
        "gy",
        split_axis=3,
        concat_axis=3,
        tiled=True,
    )
    obs_equiv = arrived.reshape(CAP, record_len, device_total)
    return (increments, height, obs_equiv)


def solution(mesh):
    return jax.shard_map(
        body,
        mesh=mesh,
        in_specs=(
            P(None, None, None, "gy", "gx"),
            P(None, None, "gy", "gx"),
            P(None, "gy", "gx"),
            P(None, "gy", "gx"),
            P("gy", "gx"),
            P("gx", None),
            P("gx", None),
            P(),
            P(("gx", "gy"), None),
            P(("gx", "gy")),
            P(None, ("gx", "gy")),
            P(("gx", "gy")),
        ),
        out_specs=(
            P(None, None, None, "gy", "gx"),
            P(None, "gy", "gx"),
            P(None, None, ("gx", "gy")),
        ),
        check_vma=False,
    )
```

profile of v0, /device:TPU:1, one launch (start us, length us, event | category | flops | bytes accessed | tf_op | source)
XLA Modules:
  0.0 489.2 jit_solution(15231277766906948029)
XLA Ops:
  8.6 0.9 fusion.57
  9.6 51.3 %all-gather.4.cloned.1.call-done = f32[12,48,3072]{2,1,0:T(8,128)} async-done(((f32[12,48,384]{2,1,0:T(8,128)}), f32[12,48,3072]{2,1,0:T(8,128)}) %all-gather.4.cloned.1.call-update) | async-done | bytes 7077904 | tf_op jit(solution)/shard_map/all_gather | solution.py:55
  60.9 15.1 %fusion.11 = f32[12,384,48]{1,2,0:T(8,128)} fusion(f32[12,48,3072]{2,1,0:T(8,128)} %all-gather.4.cloned.1.call-done, f32[384,3072]{1,0:T(8,128)} %param.17, f32[384,48]{0,1:T(8,128)S(1)} %get-tuple-element.41), kind=kOutput, calls=%fused_computation.16 | convolution fusion | flops 8153948160 | bytes 12754944 | tf_op jit(solution)/shard_map/fyb,ab->fya/dot_general | solution.py:53
  76.0 2.4 copy.92
  78.4 3.3 reshape.729
  81.7 42.5 %all_to_all.82 = f32[32,1,6912]{2,1,0:T(1,128)S(1)} all-to-all(f32[32,1,6912]{2,1,0:T(1,128)} %reshape.729), channel_id=1, replica_groups=mesh['gx'=8,'gy'=32] {'gy'}, dimensions={0} | all-to-all | bytes 1769472 | tf_op jit(solution)/shard_map/all_to_all | solution.py:60
  124.7 3.8 reduce.1
  128.5 2.9 reshape.730
  131.4 2.8 copy.94
  134.2 3.1 all_to_all.61
  137.4 12.0 %fusion.2 = f32[12,12,1536]{2,1,0:T(8,128)S(1)} fusion(f32[12,12,1536]{2,1,0:T(8,128)S(1)} %all_to_all.61, f32[1536,1536]{1,0:T(8,128)} %all-gather.6.cloned.1.call-done), kind=kOutput, calls=%fused_computation.7 | convolution fusion | flops 4076863488 | bytes 11206656 | tf_op jit(solution)/shard_map/fxb,ab->fxa/dot_general | solution.py:61
  149.4 8.6 %copy.95 = f32[12,12,1536]{1,0,2:T(8,128)} copy(f32[12,12,1536]{2,1,0:T(8,128)S(1)} %fusion.2) | data formatting | bytes 1769472 | tf_op jit(solution)/shard_map/fxb,ab->fxa/dot_general | solution.py:61
  158.0 10.0 %reshape.731 = f32[32,1,6912]{2,1,0:T(1,128)} reshape(f32[1536,12,12]{2,1,0:T(8,128)} %bitcast.172) | data formatting | bytes 1769472
  168.0 8.0 %all-to-all-start.1 = ((f32[32,1,6912]{2,1,0:T(1,128)}), f32[32,1,6912]{2,1,0:T(1,128)S(1)}, u32[]{:S(2)}, u32[]{:S(2)}) async-start(f32[32,1,6912]{2,1,0:T(1,128)} %reshape.731), calls=%async_computation.1 | async-start | bytes 1769472 | tf_op jit(solution)/shard_map/all_to_all | solution.py:62
  176.1 0.8 copy.91
  176.9 0.7 negate_divide_fusion.2
  177.6 0.7 multiply_add_fusion
  179.6 0.7 slice_bitcast_fusion.5
  180.4 17.1 %all-to-all-done.1 = f32[32,1,6912]{2,1,0:T(1,128)S(1)} async-done(((f32[32,1,6912]{2,1,0:T(1,128)}), f32[32,1,6912]{2,1,0:T(1,128)S(1)}, u32[]{:S(2)}, u32[]{:S(2)}) %all-to-all-start.1) | async-done | bytes 884768 | tf_op jit(solution)/shard_map/all_to_all | solution.py:62
  197.4 2.7 reduce.2
  200.2 8.0 %reshape.732 = f32[1536,12,12]{2,1,0:T(8,128)} reshape(f32[32,6912]{1,0:T(8,128)S(1)} %reduce.2) | data formatting | bytes 1769472
  208.2 9.7 %copy.96 = f32[12,12,32,48]{3,1,2,0:T(8,128)S(1)} copy(f32[12,12,32,48]{1,0,3,2:T(8,128)} %bitcast.174) | data formatting | bytes 1769472 | tf_op jit(solution)/shard_map/all_to_all | solution.py:62
  217.9 1.6 all_to_all.65
  219.4 1.8 bitcast_multiply_fusion.1
  221.3 0.9 copy.97
  222.2 1.5 subtract_dynamic-update-slice_fusion.1
  223.7 0.9 constant_dynamic-update-slice_fusion.3
  224.7 0.9 copy-done.1
  225.6 46.7 %all-gather.8.cloned.1.call-done = f32[12,48,3072]{2,1,0:T(8,128)} async-done(((f32[12,48,384]{2,1,0:T(8,128)}), f32[12,48,3072]{2,1,0:T(8,128)}) %all-gather.8.cloned.1.call-update) | async-done | bytes 7077904 | tf_op jit(solution)/shard_map/all_gather | solution.py:55
  272.4 15.1 %fusion.17 = f32[12,384,48]{1,2,0:T(8,128)} fusion(f32[12,48,3072]{2,1,0:T(8,128)} %all-gather.8.cloned.1.call-done, f32[384,3072]{1,0:T(8,128)} %param.17, f32[384,48]{0,1:T(8,128)S(1)} %copy-done.8), kind=kOutput, calls=%fused_computation.18 | convolution fusion | flops 8153948160 | bytes 12754944 | tf_op jit(solution)/shard_map/fyb,ab->fya/dot_general | solution.py:53
  287.5 2.3 copy.98
  289.8 3.3 reshape.733
  293.1 9.7 %all-to-all-start.2 = ((f32[32,1,6912]{2,1,0:T(1,128)}), f32[32,1,6912]{2,1,0:T(1,128)S(1)}, u32[]{:S(2)}, u32[]{:S(2)}) async-start(f32[32,1,6912]{2,1,0:T(1,128)} %reshape.733), calls=%async_computation.2 | async-start | bytes 1769472 | tf_op jit(solution)/shard_map/all_to_all | solution.py:60
  303.9 20.3 %all-to-all-done.2 = f32[32,1,6912]{2,1,0:T(1,128)S(1)} async-done(((f32[32,1,6912]{2,1,0:T(1,128)}), f32[32,1,6912]{2,1,0:T(1,128)S(1)}, u32[]{:S(2)}, u32[]{:S(2)}) %all-to-all-start.2) | async-done | bytes 884768 | tf_op jit(solution)/shard_map/all_to_all | solution.py:60
  324.2 3.8 reduce.3
  328.0 2.9 reshape.734
  330.9 2.8 copy.100
  333.7 3.1 all_to_all.69
  336.8 12.0 %fusion = f32[12,12,1536]{2,1,0:T(8,128)S(1)} fusion(f32[12,12,1536]{2,1,0:T(8,128)S(1)} %all_to_all.69, f32[1536,1536]{1,0:T(8,128)} %all-gather.6.cloned.1.call-done), kind=kOutput, calls=%fused_computation.5 | convolution fusion | flops 4076863488 | bytes 11206656 | tf_op jit(solution)/shard_map/fxb,ab->fxa/dot_general | solution.py:61
  348.8 8.8 %copy.101 = f32[12,12,1536]{1,0,2:T(8,128)} copy(f32[12,12,1536]{2,1,0:T(8,128)S(1)} %fusion) | data formatting | bytes 1769472 | tf_op jit(solution)/shard_map/fxb,ab->fxa/dot_general | solution.py:61
  357.7 10.0 %reshape.735 = f32[32,1,6912]{2,1,0:T(1,128)} reshape(f32[1536,12,12]{2,1,0:T(8,128)} %bitcast.173) | data formatting | bytes 1769472
  367.7 8.4 %all-to-all-start.3 = ((f32[32,1,6912]{2,1,0:T(1,128)}), f32[32,1,6912]{2,1,0:T(1,128)S(1)}, u32[]{:S(2)}, u32[]{:S(2)}) async-start(f32[32,1,6912]{2,1,0:T(1,128)} %reshape.735), calls=%async_computation.3 | async-start | bytes 1769472 | tf_op jit(solution)/shard_map/all_to_all | solution.py:62
  376.5 21.0 %all-to-all-done.3 = f32[32,1,6912]{2,1,0:T(1,128)S(1)} async-done(((f32[32,1,6912]{2,1,0:T(1,128)}), f32[32,1,6912]{2,1,0:T(1,128)S(1)}, u32[]{:S(2)}, u32[]{:S(2)}) %all-to-all-start.3) | async-done | bytes 884768 | tf_op jit(solution)/shard_map/all_to_all | solution.py:62
  397.5 2.8 reduce.4
  400.3 7.6 %reshape.736 = f32[1536,12,12]{2,1,0:T(8,128)} reshape(f32[32,6912]{1,0:T(8,128)S(1)} %reduce.4) | data formatting | bytes 1769472
  407.9 9.7 %copy.102 = f32[12,12,32,48]{3,1,2,0:T(8,128)S(1)} copy(f32[12,12,32,48]{1,0,3,2:T(8,128)} %bitcast.175) | data formatting | bytes 1769472 | tf_op jit(solution)/shard_map/all_to_all | solution.py:62
  417.6 1.6 all_to_all.73
  419.1 1.9 bitcast_multiply_fusion
  421.0 0.9 copy.103
  421.9 1.6 subtract_dynamic-update-slice_fusion
  423.5 0.9 constant_dynamic-update-slice_fusion.8
  424.9 5.7 %copy.106 = f32[1,13,48,384]{1,3,2,0:T(8,128)} copy(f32[1,13,48,384]{3,2,1,0:T(8,128)S(1)} %pad_maximum_fusion) | data formatting | bytes 1916928 | tf_op jit(solution)/shard_map/concatenate | solution.py:75
  430.6 2.3 gather_fusion.1
  433.0 2.3 gather_fusion.2
  435.4 2.3 gather_fusion.3
  437.8 2.3 gather_fusion
  440.4 12.1 %scatter_fusion = f32[2,13,256]{1,2,0:T(8,128)S(1)} fusion(f32[2,13,256]{1,2,0:T(8,128)S(1)} %broadcast_in_dim.15, s32[256]{0:T(256)S(1)} %bitcast.176, f32[256,13]{1,0:T(8,128)S(1)} %copy.111), kind=kCustom, calls=%fused_computation.4 | custom fusion | bytes 41984 | tf_op jit(solution)/shard_map/scatter | solution.py:103
  452.8 12.6 %all_to_all.83 = f32[8,1,832]{2,1,0:T(1,128)S(1)} all-to-all(f32[8,1,832]{2,1,0:T(1,128)S(1)} %reshape.737), channel_id=1, replica_groups=mesh['gx'=8,'gy'=32] {'gx'}, dimensions={0} | all-to-all | bytes 53248 | tf_op jit(solution)/shard_map/all_to_all | solution.py:107
  466.4 0.8 reshape.739
  467.2 4.5 all-to-all-start.5
  471.7 1.0 pad_maximum_fusion.1
  472.7 7.8 %all-to-all-done.5 = f32[32,1,208]{2,1,0:T(1,128)S(1)} async-done(((f32[32,1,208]{2,1,0:T(1,128)}), f32[32,1,208]{2,1,0:T(1,128)S(1)}, u32[]{:S(2)}, u32[]{:S(2)}) %all-to-all-start.5) | async-done | bytes 26656 | tf_op jit(solution)/shard_map/all_to_all | solution.py:106
  480.5 0.7 reduce.6
  481.6 0.7 reshape.656
  (81 shorter events, 6.7 us)
Async XLA Ops:
  7.2 53.7 %all-gather.4.cloned.1.call-start = ((), (), s32[]{:S(2)}) async-start(), calls=%async_computation.6 | async-start | bytes 7962624 | tf_op jit(solution)/shard_map/all_gather | solution.py:55
  7.9 129.5 %all-gather.6.cloned.1.call-start = ((), (), s32[]{:S(2)}) async-start(), calls=%async_computation.7 | async-start | bytes 10616832 | tf_op jit(solution)/shard_map/all_gather | solution.py:51
  9.5 51.3 %copy-start.7 = (f32[384,48]{0,1:T(8,128)}, f32[384,48]{0,1:T(8,128)S(1)}, u32[]{:S(2)}) copy-start(f32[384,48]{0,1:T(8,128)S(1)} %get-tuple-element.41) | copy-start | bytes 221188
  158.0 18.9 %copy-start = (f32[5,48,384]{2,1,0:T(8,128)S(1)}, f32[5,48,384]{2,1,0:T(8,128)}, u32[]{:S(2)}) copy-start(f32[5,48,384]{2,1,0:T(8,128)} %param.14) | copy-start | bytes 1105924
  168.0 29.5 %all-to-all-start.1 = ((f32[32,1,6912]{2,1,0:T(1,128)}), f32[32,1,6912]{2,1,0:T(1,128)S(1)}, u32[]{:S(2)}, u32[]{:S(2)}) async-start(f32[32,1,6912]{2,1,0:T(1,128)} %reshape.731), calls=%async_computation.1 | async-start | bytes 1769472 | tf_op jit(solution)/shard_map/all_to_all | solution.py:62
  176.0 96.3 %all-gather.8.cloned.1.call-start = ((), (), s32[]{:S(2)}) async-start(), calls=%async_computation.8 | async-start | bytes 7962624 | tf_op jit(solution)/shard_map/all_gather | solution.py:55
  177.6 2.8 copy-start.3
  178.3 0.6 copy-start.2
  222.2 50.2 %copy-start.8 = (f32[384,48]{0,1:T(8,128)S(1)}, f32[384,48]{0,1:T(8,128)}, u32[]{:S(2)}) copy-start(f32[384,48]{0,1:T(8,128)} %copy-done.7) | copy-start | bytes 221188
  224.7 0.9 copy-start.1
  287.5 16.0 %copy-start.11 = (s32[256,1]{0,1:T(1,128)S(1)}, s32[256,1]{0,1:T(1,128)}, u32[]{:S(2)}) copy-start(s32[256,1]{0,1:T(1,128)} %param.20) | copy-start | bytes 3076
  293.1 31.1 %all-to-all-start.2 = ((f32[32,1,6912]{2,1,0:T(1,128)}), f32[32,1,6912]{2,1,0:T(1,128)S(1)}, u32[]{:S(2)}, u32[]{:S(2)}) async-start(f32[32,1,6912]{2,1,0:T(1,128)} %reshape.733), calls=%async_computation.2 | async-start | bytes 1769472 | tf_op jit(solution)/shard_map/all_to_all | solution.py:60
  303.8 20.4 %copy-start.4 = (s32[256,2,128]{0,1,2:T(2,128)}, s32[256,2,128]{0,1,2:T(2,128)S(1)}, u32[]{:S(2)}) copy-start(s32[256,2,128]{0,1,2:T(2,128)S(1)} %fusion.23) | copy-start | bytes 786436
  303.9 29.8 %copy-start.12 = (s32[256,3]{0,1:T(4,128)}, s32[256,3]{0,1:T(4,128)S(1)}, u32[]{:S(2)}) copy-start(s32[256,3]{0,1:T(4,128)S(1)} %reduce-window.9) | copy-start | bytes 9220
  357.7 18.4 %slice-start = ((s32[256,3]{0,1:T(4,128)}), s32[256,2]{0,1:T(2,128)S(1)}, s32[]{:S(2)}) async-start(s32[256,3]{0,1:T(4,128)} %copy-done.12), calls=%async_computation.9 | async-start | bytes 4096 | tf_op jit(solution)/shard_map/slice.1
  357.7 18.4 %copy-start.5 = (s32[256,2,128]{0,1,2:T(2,128)S(1)}, s32[256,2,128]{0,1,2:T(2,128)}, u32[]{:S(2)}) copy-start(s32[256,2,128]{0,1,2:T(2,128)} %copy-done.4) | copy-start | bytes 786436
  357.7 18.7 %copy-start.15 = (f32[2,6]{1,0:T(2,128)S(1)}, f32[2,6]{1,0:T(2,128)}, u32[]{:S(2)}) copy-start(f32[2,6]{1,0:T(2,128)} %param.19) | copy-start | bytes 148
  357.7 18.7 %copy-start.13 = (s32[256]{0:T(256)S(1)}, s32[256]{0:T(256)}, u32[]{:S(2)}) copy-start(s32[256]{0:T(256)} %param.21) | copy-start | bytes 3076
  357.7 18.7 %copy-start.14 = (f32[2,256]{1,0:T(2,128)S(1)}, f32[2,256]{1,0:T(2,128)}, u32[]{:S(2)}) copy-start(f32[2,256]{1,0:T(2,128)} %param.22) | copy-start | bytes 6148
  367.7 29.8 %all-to-all-start.3 = ((f32[32,1,6912]{2,1,0:T(1,128)}), f32[32,1,6912]{2,1,0:T(1,128)S(1)}, u32[]{:S(2)}, u32[]{:S(2)}) async-start(f32[32,1,6912]{2,1,0:T(1,128)} %reshape.735), calls=%async_computation.3 | async-start | bytes 1769472 | tf_op jit(solution)/shard_map/all_to_all | solution.py:62
  421.9 2.6 copy-start.6
  421.9 2.6 copy-start.9
  424.8 5.8 %copy-start.10 = (f32[48,384]{1,0:T(8,128)}, f32[48,384]{1,0:T(8,128)S(1)}, u32[]{:S(2)}) copy-start(f32[48,384]{1,0:T(8,128)S(1)} %get-tuple-element.11) | copy-start | bytes 221188
  467.2 13.2 %all-to-all-start.5 = ((f32[32,1,208]{2,1,0:T(1,128)}), f32[32,1,208]{2,1,0:T(1,128)S(1)}, u32[]{:S(2)}, u32[]{:S(2)}) async-start(f32[32,1,208]{2,1,0:T(1,128)} %reshape.739), calls=%async_computation.5 | async-start | bytes 65536 | tf_op jit(solution)/shard_map/all_to_all | solution.py:106
Sparse Core Ops, SparseCore 0:
  9.8 51.0 all-gather.3
  62.7 56.8 all-gather.5
  225.8 46.5 all-gather.7
where the time goes:
time: 498 us; the launch traced here: 489 us
  waiting for transfers between devices  166 us (33%)
  local copies, waits for them, and re-layouts  140 us (28%)
  blocking collectives  55.1 us (11%)
  matrix products  54.3 us (11%)
  starting transfers between devices  30.7 us (6%)
  other arithmetic  28 us (6%)
  between operations  15.3 us (3%)
    all_gather x2, waiting for transfers between devices, body(): lax.all_gather(grid_field, 'gx', axis=2, tiled=True)  98 us
    unnamed x49, local copies, waits for them, and re-layouts  50.9 us
    all_to_all x1, blocking collectives, body(): lax.all_to_all(turned, 'gy', split_axis=1, concat_axis=2, tiled=True)  42.5 us
    all_to_all x2, waiting for transfers between devices, body(): lax.all_to_all(solved, 'gy', split_axis=2, concat_axis=1, tiled=True)  38.1 us
    dot_general x2, matrix products, body(): jnp.einsum('fyb,ab->fya', lax.all_gather(grid_field, 'gx', axis=2, tiled=...  30.3 us
    dot_general x2, matrix products, body(): solved = jnp.einsum('fxb,ab->fxa', merid_lines, whole_y, precision=highest)  24 us
    all_to_all x4, local copies, waits for them, and re-layouts, body(): lax.all_to_all(solved, 'gy', split_axis=2, concat_axis=1, tiled=True)  22.5 us
    all_to_all x1, waiting for transfers between devices, body(): lax.all_to_all(turned, 'gy', split_axis=1, concat_axis=2, tiled=True)  20.3 us
  transfers between devices with their start and end apart: 7, of which 6 were waited for; matrix products, arithmetic and copies ran while one was open for 8% of the time, Pallas kernels for 0%

commit v1 on v0

--- a/solution.py
+++ b/solution.py
@@ -50,11 +50,14 @@
     grid_field = control.reshape(field_count, lat_rows, lon_cols)
     whole_y = lax.all_gather(y_inverse, "gx", axis=0, tiled=True)
     for diffusion_step in range(STEPS):
+        link_rails_by_axis = lambda message, which_axis: jnp.concatenate(
+            lax.all_to_all(
+                jnp.stack(lax.axis_size(which_axis) * [message], axis=0), which_axis, 0, 0
+            ),
+            axis=2,
+        )
         grid_field = sea_open * jnp.einsum(
-            "fyb,ab->fya",
-            lax.all_gather(grid_field, "gx", axis=2, tiled=True),
-            x_inverse,
-            precision=highest,
+            "fyb,ab->fya", link_rails_by_axis(grid_field, "gx"), x_inverse, precision=highest
         )
         turned = jnp.swapaxes(grid_field, 1, 2)
         merid_lines = lax.all_to_all(turned, "gy", split_axis=1, concat_axis=2, tiled=True)

time: 498 us -> 603 us (1.21)
  blocking collectives: 55.1 us -> 132 us
  waiting for transfers between devices: 166 us -> 185 us
  local copies, waits for them, and re-layouts: 140 us -> 149 us
    all_to_all x0 -> x1, waiting for transfers between devices: none -> 118 us  [body(): lax.all_to_all(jnp.stack(lax.axis_size(which_axis) * [message], axis=0),...]
    all_gather x2 -> x0, waiting for transfers between devices: 98 us -> none  [body(): lax.all_gather(grid_field, 'gx', axis=2, tiled=True)]
    all_to_all x0 -> x1, blocking collectives: none -> 88.6 us  [body(): lax.all_to_all(jnp.stack(lax.axis_size(which_axis) * [message], axis=0),...]
    all_to_all x1, blocking collectives: 42.5 us -> 31 us  [body(): lax.all_to_all(turned, 'gy', split_axis=1, concat_axis=2, tiled=True)]
    all_to_all x0 -> x1, starting transfers between devices: none -> 8.07 us  [body(): lax.all_to_all(jnp.stack(lax.axis_size(which_axis) * [message], axis=0),...]
    unnamed x49 -> x53, local copies, waits for them, and re-layouts: 50.9 us -> 49.9 us
  transfers between devices with their start and end apart: 7 -> 6, of which waited for: 6 -> 5; matrix products, arithmetic and copies ran while one was open for 8% -> 7% of each run, Pallas kernels for 0% -> 0%
where the time goes in v1:
time: 603 us; the launch traced here: 593 us
  waiting for transfers between devices  185 us (31%)
  local copies, waits for them, and re-layouts  149 us (25%)
  blocking collectives  132 us (22%)
  matrix products  50.5 us (8%)
  starting transfers between devices  34.5 us (6%)
  other arithmetic  27.1 us (4%)
  between operations  15.4 us (3%)
    all_to_all x1, waiting for transfers between devices, body(): lax.all_to_all(jnp.stack(lax.axis_size(which_axis) * [message], axis=0),...  118 us
    all_to_all x1, blocking collectives, body(): lax.all_to_all(jnp.stack(lax.axis_size(which_axis) * [message], axis=0),...  88.6 us
    unnamed x53, local copies, waits for them, and re-layouts  49.9 us
    all_to_all x2, waiting for transfers between devices, body(): lax.all_to_all(solved, 'gy', split_axis=2, concat_axis=1, tiled=True)  38.2 us
    all_to_all x1, blocking collectives, body(): lax.all_to_all(turned, 'gy', split_axis=1, concat_axis=2, tiled=True)  31 us
    dot_general x2, matrix products, body(): jnp.einsum('fyb,ab->fya', link_rails_by_axis(grid_field, 'gx'), x_inverse...  26.6 us
    dot_general x2, matrix products, body(): solved = jnp.einsum('fxb,ab->fxa', merid_lines, whole_y, precision=highest)  24 us
    all_to_all x4, local copies, waits for them, and re-layouts, body(): lax.all_to_all(solved, 'gy', split_axis=2, concat_axis=1, tiled=True)  22.5 us
  transfers between devices with their start and end apart: 6, of which 5 were waited for; matrix products, arithmetic and copies ran while one was open for 7% of the time, Pallas kernels for 0%

profile of v1, /device:TPU:1, one launch (start us, length us, event | category | flops | bytes accessed | tf_op | source)
XLA Modules:
  0.0 593.3 jit_solution(5878513302031680493)
XLA Ops:
  7.9 4.6 stack.14
  12.5 8.1 %all-to-all-start = ((f32[8,12,48,384]{3,2,1,0:T(8,128)}), f32[8,12,48,384]{3,2,1,0:T(8,128)}, u32[]{:S(2)}, u32[]{:S(2)}) async-start(f32[8,12,48,384]{3,2,1,0:T(8,128)} %stack.14), calls=%async_computation | async-start | bytes 14155776 | tf_op jit(solution)/shard_map/all_to_all | solution.py:54
  20.6 117.7 %all-to-all-done = f32[8,12,48,384]{3,2,1,0:T(8,128)} async-done(((f32[8,12,48,384]{3,2,1,0:T(8,128)}), f32[8,12,48,384]{3,2,1,0:T(8,128)}, u32[]{:S(2)}, u32[]{:S(2)}) %all-to-all-start) | async-done | bytes 7077920 | tf_op jit(solution)/shard_map/all_to_all | solution.py:54
  138.3 4.0 copy.124
  142.3 14.1 %fusion.11 = f32[12,384,48]{1,2,0:T(8,128)} fusion(f32[12,48,3072]{2,1,0:T(8,128)S(1)} %bitcast.184, f32[384,3072]{1,0:T(8,128)} %param.17, f32[384,48]{0,1:T(8,128)S(1)} %get-tuple-element.41), kind=kOutput, calls=%fused_computation.16 | convolution fusion | flops 8153948160 | bytes 12754944 | tf_op jit(solution)/shard_map/fyb,ab->fya/dot_general | solution.py:59
  156.4 2.3 copy.96
  158.8 3.3 reshape.741
  162.1 31.0 %all_to_all.92 = f32[32,1,6912]{2,1,0:T(1,128)S(1)} all-to-all(f32[32,1,6912]{2,1,0:T(1,128)} %reshape.741), channel_id=1, replica_groups=mesh['gx'=8,'gy'=32] {'gy'}, dimensions={0} | all-to-all | bytes 1769472 | tf_op jit(solution)/shard_map/all_to_all | solution.py:63
  193.6 3.8 reduce.1
  197.4 2.9 reshape.742
  200.3 2.9 copy.98
  203.1 3.1 all_to_all.68
  206.3 12.0 %fusion.2 = f32[12,12,1536]{2,1,0:T(8,128)S(1)} fusion(f32[12,12,1536]{2,1,0:T(8,128)S(1)} %all_to_all.68, f32[1536,1536]{1,0:T(8,128)} %all-gather.2.cloned.1.call-done), kind=kOutput, calls=%fused_computation.7 | convolution fusion | flops 4076863488 | bytes 11206656 | tf_op jit(solution)/shard_map/fxb,ab->fxa/dot_general | solution.py:64
  218.3 8.7 %copy.99 = f32[12,12,1536]{1,0,2:T(8,128)} copy(f32[12,12,1536]{2,1,0:T(8,128)S(1)} %fusion.2) | data formatting | bytes 1769472 | tf_op jit(solution)/shard_map/fxb,ab->fxa/dot_general | solution.py:64
  226.9 10.1 %reshape.743 = f32[32,1,6912]{2,1,0:T(1,128)} reshape(f32[1536,12,12]{2,1,0:T(8,128)} %bitcast.178) | data formatting | bytes 1769472
  237.0 8.4 %all-to-all-start.2 = ((f32[32,1,6912]{2,1,0:T(1,128)}), f32[32,1,6912]{2,1,0:T(1,128)S(1)}, u32[]{:S(2)}, u32[]{:S(2)}) async-start(f32[32,1,6912]{2,1,0:T(1,128)} %reshape.743), calls=%async_computation.2 | async-start | bytes 1769472 | tf_op jit(solution)/shard_map/all_to_all | solution.py:65
  245.5 0.8 copy.94
  249.0 0.7 slice_bitcast_fusion.5
  249.7 17.2 %all-to-all-done.2 = f32[32,1,6912]{2,1,0:T(1,128)S(1)} async-done(((f32[32,1,6912]{2,1,0:T(1,128)}), f32[32,1,6912]{2,1,0:T(1,128)S(1)}, u32[]{:S(2)}, u32[]{:S(2)}) %all-to-all-start.2) | async-done | bytes 884768 | tf_op jit(solution)/shard_map/all_to_all | solution.py:65
  266.9 2.7 reduce.2
  269.7 7.7 %reshape.744 = f32[1536,12,12]{2,1,0:T(8,128)} reshape(f32[32,6912]{1,0:T(8,128)S(1)} %reduce.2) | data formatting | bytes 1769472
  277.4 9.7 %copy.100 = f32[12,12,32,48]{3,1,2,0:T(8,128)S(1)} copy(f32[12,12,32,48]{1,0,3,2:T(8,128)} %bitcast.180) | data formatting | bytes 1769472 | tf_op jit(solution)/shard_map/all_to_all | solution.py:65
  287.1 1.6 all_to_all.72
  288.7 1.8 bitcast_multiply_fusion.1
  290.5 0.9 copy.101
  291.4 1.5 subtract_dynamic-update-slice_fusion.1
  292.9 0.9 constant_dynamic-update-slice_fusion.3
  294.5 88.6 %all_to_all.93 = f32[8,12,48,384]{3,2,1,0:T(8,128)S(1)} all-to-all(f32[8,12,48,384]{3,2,1,0:T(8,128)S(1)} %stack.16), channel_id=1, replica_groups=mesh['gx'=8,'gy'=32] {'gx'}, dimensions={0} | all-to-all | bytes 14155776 | tf_op jit(solution)/shard_map/all_to_all | solution.py:54
  383.1 0.9 copy.125
  384.2 12.4 %fusion.17 = f32[12,384,48]{1,2,0:T(8,128)} fusion(f32[12,48,3072]{2,1,0:T(8,128)S(1)} %bitcast.183, f32[384,3072]{1,0:T(8,128)S(1)} %bitcast.186, f32[384,48]{0,1:T(8,128)S(1)} %copy-done.7), kind=kOutput, calls=%fused_computation.18 | convolution fusion | flops 8153948160 | bytes 12754944 | tf_op jit(solution)/shard_map/fyb,ab->fya/dot_general | solution.py:59
  396.6 2.3 copy.103
  399.0 3.3 reshape.745
  402.3 4.9 all-to-all-start.4
  408.2 20.3 %all-to-all-done.4 = f32[32,1,6912]{2,1,0:T(1,128)S(1)} async-done(((f32[32,1,6912]{2,1,0:T(1,128)}), f32[32,1,6912]{2,1,0:T(1,128)S(1)}, u32[]{:S(2)}, u32[]{:S(2)}) %all-to-all-start.4) | async-done | bytes 884768 | tf_op jit(solution)/shard_map/all_to_all | solution.py:63
  428.6 3.8 reduce.3
  432.4 2.9 reshape.746
  435.2 2.9 copy.105
  438.1 3.1 all_to_all.77
  441.2 12.0 %fusion = f32[12,12,1536]{2,1,0:T(8,128)S(1)} fusion(f32[12,12,1536]{2,1,0:T(8,128)S(1)} %all_to_all.77, f32[1536,1536]{1,0:T(8,128)} %all-gather.2.cloned.1.call-done), kind=kOutput, calls=%fused_computation.5 | convolution fusion | flops 4076863488 | bytes 11206656 | tf_op jit(solution)/shard_map/fxb,ab->fxa/dot_general | solution.py:64
  453.2 8.7 %copy.106 = f32[12,12,1536]{1,0,2:T(8,128)} copy(f32[12,12,1536]{2,1,0:T(8,128)S(1)} %fusion) | data formatting | bytes 1769472 | tf_op jit(solution)/shard_map/fxb,ab->fxa/dot_general | solution.py:64
  462.0 10.0 %reshape.747 = f32[32,1,6912]{2,1,0:T(1,128)} reshape(f32[1536,12,12]{2,1,0:T(8,128)} %bitcast.179) | data formatting | bytes 1769472
  472.0 8.5 %all-to-all-start.5 = ((f32[32,1,6912]{2,1,0:T(1,128)}), f32[32,1,6912]{2,1,0:T(1,128)S(1)}, u32[]{:S(2)}, u32[]{:S(2)}) async-start(f32[32,1,6912]{2,1,0:T(1,128)} %reshape.747), calls=%async_computation.5 | async-start | bytes 1769472 | tf_op jit(solution)/shard_map/all_to_all | solution.py:65
  480.9 21.0 %all-to-all-done.5 = f32[32,1,6912]{2,1,0:T(1,128)S(1)} async-done(((f32[32,1,6912]{2,1,0:T(1,128)}), f32[32,1,6912]{2,1,0:T(1,128)S(1)}, u32[]{:S(2)}, u32[]{:S(2)}) %all-to-all-start.5) | async-done | bytes 884768 | tf_op jit(solution)/shard_map/all_to_all | solution.py:65
  501.9 2.8 reduce.4
  504.7 7.7 %reshape.748 = f32[1536,12,12]{2,1,0:T(8,128)} reshape(f32[32,6912]{1,0:T(8,128)S(1)} %reduce.4) | data formatting | bytes 1769472
  512.5 9.7 %copy.107 = f32[12,12,32,48]{3,1,2,0:T(8,128)S(1)} copy(f32[12,12,32,48]{1,0,3,2:T(8,128)} %bitcast.181) | data formatting | bytes 1769472 | tf_op jit(solution)/shard_map/all_to_all | solution.py:65
  522.1 1.6 all_to_all.81
  523.7 1.9 bitcast_multiply_fusion
  525.6 0.9 copy.108
  526.5 1.6 subtract_dynamic-update-slice_fusion
  528.1 0.9 constant_dynamic-update-slice_fusion.8
  529.4 5.7 copy.111
  535.1 2.3 gather_fusion.1
  537.5 2.3 gather_fusion.2
  539.9 2.4 gather_fusion.3
  542.3 2.3 gather_fusion
  544.9 12.1 %scatter_fusion = f32[2,13,256]{1,2,0:T(8,128)S(1)} fusion(f32[2,13,256]{1,2,0:T(8,128)S(1)} %broadcast_in_dim.15, s32[256]{0:T(256)S(1)} %bitcast.187, f32[256,13]{1,0:T(8,128)S(1)} %copy.116), kind=kCustom, calls=%fused_computation.4 | custom fusion | bytes 41984 | tf_op jit(solution)/shard_map/scatter | solution.py:106
  557.4 12.0 %all_to_all.94 = f32[8,1,832]{2,1,0:T(1,128)S(1)} all-to-all(f32[8,1,832]{2,1,0:T(1,128)S(1)} %reshape.749), channel_id=1, replica_groups=mesh['gx'=8,'gy'=32] {'gx'}, dimensions={0} | all-to-all | bytes 53248 | tf_op jit(solution)/shard_map/all_to_all | solution.py:110
  570.4 0.8 reshape.751
  571.2 4.5 all-to-all-start.7
  575.7 1.0 pad_maximum_fusion.1
  576.7 7.8 %all-to-all-done.7 = f32[32,1,208]{2,1,0:T(1,128)S(1)} async-done(((f32[32,1,208]{2,1,0:T(1,128)}), f32[32,1,208]{2,1,0:T(1,128)S(1)}, u32[]{:S(2)}, u32[]{:S(2)}) %all-to-all-start.7) | async-done | bytes 26656 | tf_op jit(solution)/shard_map/all_to_all | solution.py:109
  584.5 0.7 reduce.6
  585.6 0.7 reshape.668
  (87 shorter events, 8.1 us)
Async XLA Ops:
  7.2 199.1 %all-gather.2.cloned.1.call-start = ((), (), s32[]{:S(2)}) async-start(), calls=%async_computation.8 | async-start | bytes 10616832 | tf_op jit(solution)/shard_map/all_gather | solution.py:51
  12.5 8.1 %copy-start.10 = (s32[48,384]{1,0:T(8,128)S(1)}, s32[48,384]{1,0:T(8,128)}, u32[]{:S(2)}) copy-start(s32[48,384]{1,0:T(8,128)} %param.16) | copy-start | bytes 221188
  12.5 125.8 %all-to-all-start = ((f32[8,12,48,384]{3,2,1,0:T(8,128)}), f32[8,12,48,384]{3,2,1,0:T(8,128)}, u32[]{:S(2)}, u32[]{:S(2)}) async-start(f32[8,12,48,384]{3,2,1,0:T(8,128)} %stack.14), calls=%async_computation | async-start | bytes 14155776 | tf_op jit(solution)/shard_map/all_to_all | solution.py:54
  20.6 121.7 %copy-start.6 = (f32[384,48]{0,1:T(8,128)}, f32[384,48]{0,1:T(8,128)S(1)}, u32[]{:S(2)}) copy-start(f32[384,48]{0,1:T(8,128)S(1)} %get-tuple-element.41) | copy-start | bytes 221188
  226.9 19.4 %copy-start = (f32[5,48,384]{2,1,0:T(8,128)S(1)}, f32[5,48,384]{2,1,0:T(8,128)}, u32[]{:S(2)}) copy-start(f32[5,48,384]{2,1,0:T(8,128)} %param.14) | copy-start | bytes 1105924
  237.0 29.9 %all-to-all-start.2 = ((f32[32,1,6912]{2,1,0:T(1,128)}), f32[32,1,6912]{2,1,0:T(1,128)S(1)}, u32[]{:S(2)}, u32[]{:S(2)}) async-start(f32[32,1,6912]{2,1,0:T(1,128)} %reshape.743), calls=%async_computation.2 | async-start | bytes 1769472 | tf_op jit(solution)/shard_map/all_to_all | solution.py:65
  247.0 2.7 copy-start.2
  247.7 0.6 copy-start.1
  294.5 89.6 %slice-start = ((s8[4718592]{0:T(1024)(128)(4,1)}), s8[4194304]{0:T(1024)(128)(4,1)S(1)}, s32[]{:S(2)}) async-start(s8[4718592]{0:T(1024)(128)(4,1)} %bitcast.185), calls=%async_computation.9 | async-start | bytes 8388608
  383.1 1.0 slice-start.1
  383.1 1.0 copy-start.7
  396.6 11.2 %copy-start.11 = (s32[256,1]{0,1:T(1,128)S(1)}, s32[256,1]{0,1:T(1,128)}, u32[]{:S(2)}) copy-start(s32[256,1]{0,1:T(1,128)} %param.20) | copy-start | bytes 3076
  402.3 26.3 %all-to-all-start.4 = ((f32[32,1,6912]{2,1,0:T(1,128)}), f32[32,1,6912]{2,1,0:T(1,128)S(1)}, u32[]{:S(2)}, u32[]{:S(2)}) async-start(f32[32,1,6912]{2,1,0:T(1,128)} %reshape.745), calls=%async_computation.4 | async-start | bytes 1769472 | tf_op jit(solution)/shard_map/all_to_all | solution.py:63
  408.2 20.4 %copy-start.3 = (s32[256,2,128]{0,1,2:T(2,128)}, s32[256,2,128]{0,1,2:T(2,128)S(1)}, u32[]{:S(2)}) copy-start(s32[256,2,128]{0,1,2:T(2,128)S(1)} %fusion.23) | copy-start | bytes 786436
  408.2 29.9 %copy-start.12 = (s32[256,3]{0,1:T(4,128)}, s32[256,3]{0,1:T(4,128)S(1)}, u32[]{:S(2)}) copy-start(s32[256,3]{0,1:T(4,128)S(1)} %reduce-window.9) | copy-start | bytes 9220
  461.9 18.5 %slice-start.2 = ((s32[256,3]{0,1:T(4,128)}), s32[256,2]{0,1:T(2,128)S(1)}, s32[]{:S(2)}) async-start(s32[256,3]{0,1:T(4,128)} %copy-done.12), calls=%async_computation.11 | async-start | bytes 4096 | tf_op jit(solution)/shard_map/slice.1
  461.9 18.5 %copy-start.4 = (s32[256,2,128]{0,1,2:T(2,128)S(1)}, s32[256,2,128]{0,1,2:T(2,128)}, u32[]{:S(2)}) copy-start(s32[256,2,128]{0,1,2:T(2,128)} %copy-done.3) | copy-start | bytes 786436
  462.0 18.8 %copy-start.15 = (f32[2,6]{1,0:T(2,128)S(1)}, f32[2,6]{1,0:T(2,128)}, u32[]{:S(2)}) copy-start(f32[2,6]{1,0:T(2,128)} %param.19) | copy-start | bytes 148
  462.0 18.8 %copy-start.13 = (s32[256]{0:T(256)S(1)}, s32[256]{0:T(256)}, u32[]{:S(2)}) copy-start(s32[256]{0:T(256)} %param.21) | copy-start | bytes 3076
  462.0 18.9 %copy-start.14 = (f32[2,256]{1,0:T(2,128)S(1)}, f32[2,256]{1,0:T(2,128)}, u32[]{:S(2)}) copy-start(f32[2,256]{1,0:T(2,128)} %param.22) | copy-start | bytes 6148
  472.0 30.0 %all-to-all-start.5 = ((f32[32,1,6912]{2,1,0:T(1,128)}), f32[32,1,6912]{2,1,0:T(1,128)S(1)}, u32[]{:S(2)}, u32[]{:S(2)}) async-start(f32[32,1,6912]{2,1,0:T(1,128)} %reshape.747), calls=%async_computation.5 | async-start | bytes 1769472 | tf_op jit(solution)/shard_map/all_to_all | solution.py:65
  526.5 2.6 copy-start.5
  526.5 2.6 copy-start.8
  529.3 5.7 copy-start.9
  571.2 13.3 %all-to-all-start.7 = ((f32[32,1,208]{2,1,0:T(1,128)}), f32[32,1,208]{2,1,0:T(1,128)S(1)}, u32[]{:S(2)}, u32[]{:S(2)}) async-start(f32[32,1,208]{2,1,0:T(1,128)} %reshape.751), calls=%async_computation.7 | async-start | bytes 65536 | tf_op jit(solution)/shard_map/all_to_all | solution.py:109
Sparse Core Ops, SparseCore 0:
  9.8 110.8 all-gather.1
